TPU v7x, 256 devices: a whole 4x4x8 slice. The times are simulated.
256 devices in a mesh: dp: 16 (over x, y), ctx: 16 (over z, core).
Axes of the slice: x: 4, y: 4, z: 8, core: 2. Of those that a mesh axis runs over, the one named last changes fastest.
Arguments:
- hidden_in: bfloat16 [16, 2048, 1536], P('dp', 'ctx'), may hold values from -12 to 12
- cotangent: bfloat16 [16, 2048, 1536], P('dp', 'ctx'), may hold values from -0.29882812 to 0.29882812
- w_qkv: bfloat16 [3, 1536, 2048], P(None, None, 'ctx'), may hold values from -1 to 1
- w_out: bfloat16 [2048, 1536], P('ctx'), may hold values from -0.125 to 0.125
- q_gain: float32 [128], replicated, may hold values from 0.1 to 1.9
- k_gain: float32 [128], replicated, may hold values from 0.1 to 1.9
- tile_list: int32 [16, 32, 32], P('ctx'), may hold values from -1 to 31, as said below
Outputs:
- layer_out: bfloat16 [16, 2048, 1536], P('dp', 'ctx')
- grad_qkv: float32 [3, 1536, 2048], P(None, None, 'ctx')
- grad_out: float32 [2048, 1536], P('ctx')
Inputs may be any that keep to these rules, and one draw needn't show every extreme that they name: tile_list[h, t] lists in increasing order the key tiles that query tile t attends to in head h, then -1 up to 32 entries. Tiles are numbered row-major over a grid of 2 x 4 x 4, tile t holding tokens t * 64 to (t + 1) * 64 - 1. Each head has a window of fixed extents in tiles along the three grid dimensions, centred on the query tile and shifted inward at the grid's edges, so that all query tiles of one head list the same number of tiles, the query tile among them. Some head's window is the whole grid.
All inputs are finite; a program needn't handle non-finite values.
Results may differ from a plain program's by a relative error of at most 0.014.
Values may be sent and summed in bfloat16 or wider, within the bound.
A program may use at most 128 MiB of HBM per device.

v0:
```python
import jax
import jax.numpy as jnp
from jax import lax
from jax.sharding import PartitionSpec as P

BLOCK = 512


EPS = 1e-06


def as_sent(value):
    return jax.tree.map(lambda a: a.astype(jnp.bfloat16) if a.dtype == jnp.float32 else a, value)


def tile_allowed(lists, tile_count):
    match = lists[:, :, None] == jnp.arange(tile_count, dtype=jnp.int32)[None, None, :]
    return jnp.any(match, axis=1).astype(jnp.float32)


def expand_rows(allowed_rows, tile_rows):
    return jnp.repeat(jnp.repeat(allowed_rows, tile_rows, axis=0), tile_rows, axis=1)


def rms_forward(raw, gain):
    inverse = lax.rsqrt(jnp.mean(raw * raw, axis=-1, keepdims=True) + EPS)
    return ((raw * inverse * gain).astype(jnp.bfloat16), inverse)


def rms_backward(raw, inverse, gain, upstream):
    normed = raw * inverse
    scaled = gain * upstream
    return (inverse * (scaled - normed * jnp.mean(normed * scaled, axis=-1, keepdims=True))).astype(
        jnp.bfloat16
    )


def contract(left, right, left_dim, right_dim):
    return lax.dot_general(
        left, right, (((left_dim,), (right_dim,)), ((), ())), preferred_element_type=jnp.float32
    )


def dot_plain(operands):
    return contract(operands[0], operands[1], 1, 0)


def zero_plain(operands):
    return jnp.zeros((operands[0].shape[0], operands[1].shape[1]), jnp.float32)


def dot_inner(operands):
    return contract(operands[0], operands[1], 1, 1)


def zero_inner(operands):
    return jnp.zeros((operands[0].shape[0], operands[1].shape[0]), jnp.float32)


def dot_outer(operands):
    return contract(operands[0], operands[1], 0, 0)


def zero_outer(operands):
    return jnp.zeros((operands[0].shape[1], operands[1].shape[1]), jnp.float32)


def per_device(hidden_in, cotangent, w_qkv, w_out, q_gain, k_gain, tile_list):
    tokens, upstream = (
        lax.all_gather(hidden_in[0], "ctx", axis=0, tiled=True),
        lax.all_gather(cotangent[0], "ctx", axis=0, tiled=True),
    )
    seq_len = tokens.shape[0]
    head_size = q_gain.shape[0]
    tile_count = tile_list.shape[1]
    tile_rows = seq_len // tile_count
    block_tiles = BLOCK // tile_rows
    block_count = seq_len // BLOCK
    score_scale = head_size ** (-0.5)
    indices = jnp.arange(block_count, dtype=jnp.int32)

    def exp_block(operands):
        return jnp.exp(contract(operands[0], operands[1], 1, 1) * score_scale) * operands[2]

    def probabilities_of(query_block, key_normed, allowed_block, active_row):
        pieces = []
        for key_index in range(block_count):
            low = key_index * BLOCK
            pieces.append(
                lax.cond(
                    active_row[key_index],
                    exp_block,
                    zero_inner,
                    (
                        query_block,
                        key_normed[low : low + BLOCK],
                        allowed_block[:, low : low + BLOCK],
                    ),
                )
            )
        weighted = jnp.concatenate(pieces, axis=1)
        return weighted / jnp.sum(weighted, axis=-1, keepdims=True)

    def block_inputs(state, index):
        query_normed, key_normed, allowed, active = (state[2], state[3], state[7], state[8])
        query_block = lax.dynamic_slice_in_dim(query_normed, index * BLOCK, BLOCK, 0)
        allowed_block = expand_rows(
            lax.dynamic_slice_in_dim(allowed, index * block_tiles, block_tiles, 0), tile_rows
        )
        active_row = active[index]
        probabilities = probabilities_of(query_block, key_normed, allowed_block, active_row)
        return (query_block, active_row, probabilities)

    head = 0
    low_col = head * head_size
    high_col = low_col + head_size
    query_raw = jnp.dot(tokens, w_qkv[0, :, low_col:high_col], preferred_element_type=jnp.float32)
    key_raw = jnp.dot(tokens, w_qkv[1, :, low_col:high_col], preferred_element_type=jnp.float32)
    value_raw = jnp.dot(tokens, w_qkv[2, :, low_col:high_col], preferred_element_type=jnp.float32)
    query_normed, query_inverse = rms_forward(query_raw, q_gain)
    key_normed, key_inverse = rms_forward(key_raw, k_gain)
    values = value_raw.astype(jnp.bfloat16)
    allowed = tile_allowed(tile_list[head], tile_count)
    active = (
        jnp.max(allowed.reshape(block_count, block_tiles, block_count, block_tiles), axis=(1, 3))
        > 0.5
    )
    state = (
        query_raw,
        key_raw,
        query_normed,
        key_normed,
        query_inverse,
        key_inverse,
        values,
        allowed,
        active,
    )

    def forward_block(index):
        query_block, active_row, probabilities = block_inputs(state, index)
        weights_bf = probabilities.astype(jnp.bfloat16)
        attn_block = jnp.zeros((BLOCK, head_size), jnp.float32)
        for key_index in range(block_count):
            low = key_index * BLOCK
            attn_block = attn_block + lax.cond(
                active_row[key_index],
                dot_plain,
                zero_plain,
                (weights_bf[:, low : low + BLOCK], state[6][low : low + BLOCK]),
            )
        return attn_block.astype(jnp.bfloat16)

    attn_blocks = lax.map(forward_block, indices)
    attention_parts = [attn_blocks.reshape(seq_len, head_size)]
    states = [state]
    attention_mine = jnp.concatenate(attention_parts, axis=1)
    proj_grad = contract(attention_mine, upstream, 0, 0)
    attention_rows = lax.all_to_all(
        as_sent(attention_mine), "ctx", split_axis=0, concat_axis=1, tiled=True
    ).astype(attention_mine.dtype)
    shard_piece = lax.all_gather(w_out, "ctx", axis=0, tiled=True)
    columns = lax.slice_in_dim(attention_rows, 0, shard_piece.shape[0], axis=1)
    mixed = jnp.zeros((attention_rows.shape[0], w_out.shape[1]), jnp.float32) + jnp.dot(
        columns, shard_piece, preferred_element_type=jnp.float32
    )
    upstream_heads = contract(upstream, w_out, 1, 1).astype(jnp.bfloat16)
    head = 0
    state = states[head]
    key_normed = state[3]
    values = state[6]

    def backward_step(running, index):
        key_grad, value_grad = running
        query_block, active_row, probabilities = block_inputs(state, index)
        weights_bf = probabilities.astype(jnp.bfloat16)
        upstream_block = lax.dynamic_slice_in_dim(upstream_heads, index * BLOCK, BLOCK, 0)
        pieces = []
        for key_index in range(block_count):
            low = key_index * BLOCK
            pieces.append(
                lax.cond(
                    active_row[key_index],
                    dot_inner,
                    zero_inner,
                    (upstream_block, values[low : low + BLOCK]),
                )
            )
        weight_grad = jnp.concatenate(pieces, axis=1)
        row_delta = jnp.sum(probabilities * weight_grad, axis=-1, keepdims=True)
        score_grad = (probabilities * (weight_grad - row_delta) * score_scale).astype(jnp.bfloat16)
        query_grad = jnp.zeros((BLOCK, head_size), jnp.float32)
        for key_index in range(block_count):
            low = key_index * BLOCK
            flag = active_row[key_index]
            value_grad = value_grad.at[key_index].add(
                lax.cond(
                    flag, dot_outer, zero_outer, (weights_bf[:, low : low + BLOCK], upstream_block)
                )
            )
            query_grad = query_grad + lax.cond(
                flag,
                dot_plain,
                zero_plain,
                (score_grad[:, low : low + BLOCK], key_normed[low : low + BLOCK]),
            )
            key_grad = key_grad.at[key_index].add(
                lax.cond(
                    flag, dot_outer, zero_outer, (score_grad[:, low : low + BLOCK], query_block)
                )
            )
        return ((key_grad, value_grad), query_grad)

    zeros = jnp.zeros((block_count, BLOCK, head_size), jnp.float32)
    (key_grad, value_grad), query_grads = lax.scan(backward_step, (zeros, zeros), indices)
    query_back = rms_backward(state[0], state[4], q_gain, query_grads.reshape(seq_len, head_size))
    key_back = rms_backward(state[1], state[5], k_gain, key_grad.reshape(seq_len, head_size))
    value_back = value_grad.reshape(seq_len, head_size).astype(jnp.bfloat16)
    grad_parts = [
        jnp.stack(
            [
                contract(tokens, query_back, 0, 0),
                contract(tokens, key_back, 0, 0),
                contract(tokens, value_back, 0, 0),
            ]
        )
    ]
    qkv_grad = jnp.concatenate(grad_parts, axis=2)
    qkv_sum, proj_sum = (
        lax.psum(qkv_grad.astype(jnp.bfloat16), "dp").astype(jnp.float32),
        lax.psum(proj_grad.astype(jnp.bfloat16), "dp").astype(jnp.float32),
    )
    return (mixed.astype(jnp.bfloat16)[None], qkv_sum, proj_sum)


def solution(mesh):
    in_specs = (
        P("dp", "ctx", None),
        P("dp", "ctx", None),
        P(None, None, "ctx"),
        P("ctx", None),
        P(),
        P(),
        P("ctx", None, None),
    )
    out_specs = (P("dp", "ctx", None), P(None, None, "ctx"), P("ctx", None))
    return jax.shard_map(
        per_device, mesh=mesh, in_specs=in_specs, out_specs=out_specs, check_vma=False
    )
```

profile of v0, /device:TPU:2, one launch (start us, length us, event | category | flops | bytes accessed | tf_op | source)
XLA Modules:
  0.0 822.1 jit_solution(80118986538315432)
XLA Ops:
  11.4 47.4 %all-gather.8.cloned.1.call-done = bf16[1,2048,1536]{2,1,0:T(8,128)(2,1)} async-done(((bf16[1,128,1536]{2,1,0:T(8,128)(2,1)}), bf16[1,2048,1536]{2,1,0:T(8,128)(2,1)}) %all-gather.8.cloned.1.call-update) | async-done | bytes 6291472 | tf_op jit(solution)/shard_map/all_gather | solution.py:70
  58.9 5.0 multiply_reduce_fusion.3
  65.3 5.0 multiply_reduce_fusion.4
  72.5 5.4 fusion.70
  77.9 27.5 %all-gather.10.cloned.1.call-done = bf16[1,2048,1536]{2,1,0:T(8,128)(2,1)} async-done(((bf16[1,128,1536]{2,1,0:T(8,128)(2,1)}), bf16[1,2048,1536]{2,1,0:T(8,128)(2,1)}) %all-gather.10.cloned.1.call-update) | async-done | bytes 6291472 | tf_op jit(solution)/shard_map/all_gather | solution.py:71
  105.4 5.4 fusion.82
  113.5 292.1 %while.36 = (s32[]{:T(128)}, f32[4,512,128]{2,1,0:T(8,128)}, f32[4,512,128]{2,1,0:T(8,128)}, f32[4,512,128]{2,1,0:T(8,128)}, s32[4]{0:T(128)}, /*index=5*/pred[4...) while((s32[]{:T(128)}, f32[4,512,128]{2,1,0:T(8,128)}, ...), condition=%wide.region_72.73_spmd, body=%wide.region_26.72_spmd.sunk | while | flops 1368062976 | bytes 136878768 | solution.py:215
  126.1 7.0 conditional.66
  126.1 5.4 copy.70
  134.4 7.1 conditional.67
  134.4 5.5 copy.71
  154.2 3.0 multiply_reduce_fusion.6
  200.3 7.0 conditional.66
  200.4 5.4 copy.70
  208.6 7.0 conditional.67
  208.7 5.4 copy.71
  228.4 3.0 multiply_reduce_fusion.6
  272.9 7.0 conditional.65
  272.9 5.4 copy.72
  284.4 7.9 conditional.64
  284.4 5.4 copy.73
  302.6 3.0 multiply_reduce_fusion.6
  344.7 7.0 conditional.65
  344.7 5.4 copy.72
  356.2 7.9 conditional.64
  356.3 5.4 copy.73
  413.5 3.9 fusion.89
  421.2 138.9 %while.35 = (s32[]{:T(128)}, bf16[4,512,128]{2,1,0:T(8,128)(2,1)}, s32[4]{0:T(128)S(1)}, pred[4,4]{1,0:T(4,128)(4,1)}, bf16[2048,128]{1,0:T(8,128)(2,1)}, /*inde...) while((s32[]{:T(128)}, bf16[4,512,128]{2,1,0:T(8,128)(2,1)}, ...), condition=%wide.region_25.26_spmd, body=%wide.region_4.25_spmd.sunk | while | flops 545521152 | bytes 63070220 | solution.py:154
  431.6 7.0 conditional.59
  431.6 5.4 copy.66
  439.3 7.0 conditional.58
  439.4 5.4 copy.67
  466.3 7.0 conditional.59
  466.3 5.4 copy.66
  474.1 7.0 conditional.58
  474.1 5.4 copy.67
  500.1 7.0 conditional.57
  500.1 5.4 copy.68
  509.8 8.0 conditional.56
  509.8 5.4 copy.69
  534.8 7.0 conditional.57
  534.8 5.4 copy.68
  544.5 8.0 conditional.56
  544.5 5.4 copy.69
  560.1 4.8 fusion.85
  564.9 168.9 %all_to_all.19 = bf16[16,128,128]{2,1,0:T(8,128)(2,1)S(1)} all-to-all(bf16[16,128,128]{2,1,0:T(8,128)(2,1)S(1)} %bitcast.195), channel_id=1, replica_groups=mesh['dp'=16,'ctx'=16] {'ctx'}, dimensions={0} | all-to-all | bytes 1048576 | tf_op jit(solution)/shard_map/all_to_all | solution.py:159
  734.1 4.6 fusion.88
  738.7 72.1 %all-reduce.3.cloned.1.call-done = (bf16[3,1536,128]{1,2,0:T(8,128)(2,1)}, bf16[128,1536]{1,0:T(8,128)(2,1)}) async-done(((bf16[3,1536,128]{1,2,0:T(8,128)(2,1)}, bf16[128,1536]{1,0:T(8,128)(2,1)}), (bf16[3,1536,128]{1,2,0:T(8,128)(2,1)}, bf16[128,1536]{1,0:T(8,128)(2,1)})) %all-reduce.3.cloned.1.call-update) | async-done | bytes 1572880 | tf_op jit(solution)/shard_map/psum | solution.py:230
  (542 shorter events, 400.1 us)
Async XLA Ops:
  7.2 51.7 %all-gather.8.cloned.1.call-start = ((), (), s32[]{:S(2)}) async-start(), calls=%async_computation.2 | async-start | bytes 6684672 | tf_op jit(solution)/shard_map/all_gather | solution.py:70
  7.9 97.5 %all-gather.10.cloned.1.call-start = ((), (), s32[]{:S(2)}) async-start(), calls=%async_computation.3 | async-start | bytes 6684672 | tf_op jit(solution)/shard_map/all_gather | solution.py:71
  8.6 725.5 %all-gather.6.cloned.1.call-start = ((), (), s32[]{:S(2)}) async-start(), calls=%async_computation.1 | async-start | bytes 6684672 | tf_op jit(solution)/shard_map/all_gather | solution.py:162
  9.4 801.5 %all-reduce.3.cloned.1.call-start = ((), (), s32[]{:S(2)}) async-start(), calls=%async_computation.4 | async-start | bytes 3145728 | tf_op jit(solution)/shard_map/psum | solution.py:230
  11.4 53.4 %copy-start.28 = (f32[128]{0:T(128)S(1)}, f32[128]{0:T(128)}, u32[]{:S(2)}) copy-start(f32[128]{0:T(128)} %param.88) | copy-start | bytes 1540
  11.4 53.8 %copy-start.19 = (bf16[3,1536,128]{2,1,0:T(8,128)(2,1)S(1)}, bf16[3,1536,128]{2,1,0:T(8,128)(2,1)}, u32[]{:S(2)}) copy-start(bf16[3,1536,128]{2,1,0:T(8,128)(2,1)} %param.85) | copy-start | bytes 3538948
  63.9 6.4 copy-start.22
  65.3 6.1 copy-start.26
  71.5 33.9 %copy-start.21 = (bf16[128,1536]{1,0:T(8,128)(2,1)S(1)}, bf16[128,1536]{1,0:T(8,128)(2,1)}, u32[]{:S(2)}) copy-start(bf16[128,1536]{1,0:T(8,128)(2,1)} %param.86) | copy-start | bytes 1179652
  113.5 11.0 %copy-start.6 = (bf16[2048,128]{1,0:T(8,128)(2,1)}, bf16[2048,128]{1,0:T(8,128)(2,1)S(1)}, u32[]{:S(2)}) copy-start(bf16[2048,128]{1,0:T(8,128)(2,1)S(1)} %get-tuple-element.1236) | copy-start | bytes 1572868 | tf_op jit(solution)/shard_map/while
  120.6 5.5 copy-start.10
  134.4 8.4 %copy-start.11 = (bf16[512,128]{1,0:T(8,128)(2,1)S(1)}, bf16[512,128]{1,0:T(8,128)(2,1)}, u32[]{:S(2)}) copy-start(bf16[512,128]{1,0:T(8,128)(2,1)} %get-tuple-element.1129) | copy-start | bytes 393220 | tf_op jit(solution)/shard_map/while
  154.2 3.7 copy-start.3
  154.2 4.1 copy-start.4
  154.2 4.0 copy-start.20
  160.4 6.7 copy-start.5
  176.4 11.4 %copy-start.7 = (bf16[2048,128]{1,0:T(8,128)(2,1)S(1)}, bf16[2048,128]{1,0:T(8,128)(2,1)}, u32[]{:S(2)}) copy-start(bf16[2048,128]{1,0:T(8,128)(2,1)} %copy-done.6) | copy-start | bytes 1572868 | tf_op jit(solution)/shard_map/while
  187.7 11.0 %copy-start.6 = (bf16[2048,128]{1,0:T(8,128)(2,1)}, bf16[2048,128]{1,0:T(8,128)(2,1)S(1)}, u32[]{:S(2)}) copy-start(bf16[2048,128]{1,0:T(8,128)(2,1)S(1)} %get-tuple-element.1236) | copy-start | bytes 1572868 | tf_op jit(solution)/shard_map/while
  194.8 5.5 copy-start.10
  208.6 8.4 %copy-start.11 = (bf16[512,128]{1,0:T(8,128)(2,1)S(1)}, bf16[512,128]{1,0:T(8,128)(2,1)}, u32[]{:S(2)}) copy-start(bf16[512,128]{1,0:T(8,128)(2,1)} %get-tuple-element.1129) | copy-start | bytes 393220 | tf_op jit(solution)/shard_map/while
  228.4 3.7 copy-start.3
  228.4 4.1 copy-start.4
  228.4 4.0 copy-start.20
  234.5 6.7 copy-start.5
  250.5 11.4 %copy-start.7 = (bf16[2048,128]{1,0:T(8,128)(2,1)S(1)}, bf16[2048,128]{1,0:T(8,128)(2,1)}, u32[]{:S(2)}) copy-start(bf16[2048,128]{1,0:T(8,128)(2,1)} %copy-done.6) | copy-start | bytes 1572868 | tf_op jit(solution)/shard_map/while
  261.9 11.0 %copy-start.6 = (bf16[2048,128]{1,0:T(8,128)(2,1)}, bf16[2048,128]{1,0:T(8,128)(2,1)S(1)}, u32[]{:S(2)}) copy-start(bf16[2048,128]{1,0:T(8,128)(2,1)S(1)} %get-tuple-element.1236) | copy-start | bytes 1572868 | tf_op jit(solution)/shard_map/while
  269.0 12.4 %copy-start.10 = (bf16[512,128]{1,0:T(8,128)(2,1)}, bf16[512,128]{1,0:T(8,128)(2,1)S(1)}, u32[]{:S(2)}) copy-start(bf16[512,128]{1,0:T(8,128)(2,1)S(1)} %get-tuple-element.1132) | copy-start | bytes 393220 | tf_op jit(solution)/shard_map/while
  302.6 3.7 copy-start.3
  302.6 4.1 copy-start.4
  302.6 4.0 copy-start.20
  308.7 6.4 copy-start.5
  324.4 9.3 %copy-start.7 = (bf16[2048,128]{1,0:T(8,128)(2,1)S(1)}, bf16[2048,128]{1,0:T(8,128)(2,1)}, u32[]{:S(2)}) copy-start(bf16[2048,128]{1,0:T(8,128)(2,1)} %copy-done.6) | copy-start | bytes 1572868 | tf_op jit(solution)/shard_map/while
  333.7 11.0 %copy-start.6 = (bf16[2048,128]{1,0:T(8,128)(2,1)}, bf16[2048,128]{1,0:T(8,128)(2,1)S(1)}, u32[]{:S(2)}) copy-start(bf16[2048,128]{1,0:T(8,128)(2,1)S(1)} %get-tuple-element.1236) | copy-start | bytes 1572868 | tf_op jit(solution)/shard_map/while
  340.8 12.4 %copy-start.10 = (bf16[512,128]{1,0:T(8,128)(2,1)}, bf16[512,128]{1,0:T(8,128)(2,1)S(1)}, u32[]{:S(2)}) copy-start(bf16[512,128]{1,0:T(8,128)(2,1)S(1)} %get-tuple-element.1132) | copy-start | bytes 393220 | tf_op jit(solution)/shard_map/while
  374.4 4.1 copy-start.4
  374.4 4.0 copy-start.20
  380.6 6.4 copy-start.5
  396.2 9.3 %copy-start.7 = (bf16[2048,128]{1,0:T(8,128)(2,1)S(1)}, bf16[2048,128]{1,0:T(8,128)(2,1)}, u32[]{:S(2)}) copy-start(bf16[2048,128]{1,0:T(8,128)(2,1)} %copy-done.6) | copy-start | bytes 1572868 | tf_op jit(solution)/shard_map/while
  405.6 5.5 copy-start.9
  405.6 5.6 copy-start.25
  405.6 5.6 copy-start.27
  405.6 7.4 copy-start.23
  405.6 7.4 copy-start.29
  408.4 9.1 %slice-start = ((s8[6291456]{0:T(1024)(128)(4,1)}), s8[2097152]{0:T(1024)(128)(4,1)S(1)}, s32[]{:S(2)}) async-start(s8[6291456]{0:T(1024)(128)(4,1)} %bitcast.190), calls=%async_computation.5 | async-start | bytes 4194304
  413.2 4.3 slice-start.1
  413.2 4.3 copy-start.15
  413.2 4.6 copy-start.17
  560.1 4.8 copy-start.18
  (21 other events, 55.2 us)
Sparse Core Ops, SparseCore 0:
  9.8 48.9 all-gather.7
  60.7 44.6 all-gather.9
  107.2 44.6 all-gather.5
  565.0 245.8 all-reduce.2
where the time goes:
time: 829 us; the launch traced here: 822 us
  local copies, waits for them, and re-layouts  192 us (23%)
  blocking collectives  169 us (20%)
  waiting for transfers between devices  149 us (18%)
  other arithmetic  125 us (15%)
  matrix products  125 us (15%)
  loops' own time  48.8 us (6%)
  between operations  14.1 us (2%)
    all_to_all x1, blocking collectives, per_device(): lax.all_to_all(as_sent(attention_mine), 'ctx', split_axis=0, concat_axis=...  169 us
    another operation x74, local copies, waits for them, and re-layouts  115 us
    dot_general x61, matrix products, contract(): lax.dot_general(left, right, (((left_dim,), (right_dim,)), ((), ())), pre...  105 us
    psum x1, waiting for transfers between devices, per_device(): lax.psum(qkv_grad.astype(jnp.bfloat16), 'dp').astype(jnp.float32)  72.1 us
    all_gather x1, waiting for transfers between devices, per_device(): lax.all_gather(hidden_in[0], 'ctx', axis=0, tiled=True)  47.4 us
    all_gather x1, waiting for transfers between devices, per_device(): lax.all_gather(cotangent[0], 'ctx', axis=0, tiled=True)  27.5 us
    scatter-add x16, other arithmetic, backward_step(): key_grad.at[key_index]  27 us
    reduce_sum x40, other arithmetic, probabilities_of(): return weighted / jnp.sum(weighted, axis=-1, keepdims=True)  26.5 us
  transfers between devices with their start and end apart: 4, of which 3 were waited for; matrix products, arithmetic and copies ran while one was open for 52% of the time, Pallas kernels for 0%

commit v1 on v0

v1 whole, which is shorter than its diff:
```python
import functools
import jax
import jax.numpy as jnp
from jax.sharding import PartitionSpec as P
from jax import lax
from jax.experimental import pallas as pl
from jax.experimental.pallas import tpu as pltpu
EPS=1e-6
F32=jnp.float32; BF=jnp.bfloat16
def mm(a,b,ca=1,cb=0):
    return lax.dot_general(a,b,(((ca,),(cb,)),((),())),preferred_element_type=F32)

def qkv_block(row, rows, tok, w, gq, gk, qraw, kraw, qn, kn, va, tile_rows):
    x=tok[pl.ds(row,rows),:]
    r=mm(x,w[...])
    hd=gq.shape[1]
    q=r[:,:hd]; k=r[:,hd:2*hd]; v=r[:,2*hd:]
    qraw[pl.ds(row,rows),:]=q
    kraw[pl.ds(row,rows),:]=k
    rq=lax.rsqrt(jnp.mean(q*q,axis=-1,keepdims=True)+EPS)
    rk=lax.rsqrt(jnp.mean(k*k,axis=-1,keepdims=True)+EPS)
    qn[pl.ds(row,rows),:hd]=(q*rq*gq[...]).astype(BF)
    kn[pl.ds(row,rows),:hd]=(k*rk*gk[...]).astype(BF)
    va[pl.ds(row,rows),:hd]=v.astype(BF)
    va[pl.ds(row,rows),hd:]=jnp.ones((rows,hd),BF)
    t=(row+lax.broadcasted_iota(jnp.int32,(rows,hd),0))//tile_rows
    lane=lax.broadcasted_iota(jnp.int32,(rows,hd),1)
    qn[pl.ds(row,rows),hd:]=jnp.where(t==lane,1.0,0.0).astype(BF)

def rms_back(raw,gain,up,axis):
    inv=lax.rsqrt(jnp.mean(raw*raw,axis=axis,keepdims=True)+EPS)
    n=raw*inv
    s=gain*up
    return inv*(s-n*jnp.mean(n*s,axis=axis,keepdims=True))

def attn_block(row, rows, first, scale, qn, kn, va, dA, qraw, gq, att, gl, dkt, dvt):
    hd=gq.shape[1]
    L2E=1.4426950408889634
    qb=qn[pl.ds(row,rows),:]
    s=mm(qb,kn[...],1,1)
    e=jnp.exp2(s*(scale*L2E))
    eb=e.astype(BF)
    av=mm(eb,va[...])
    inv=1.0/av[:,hd:]
    a=av[:,:hd]*inv
    att[pl.ds(row,rows),:]=a.astype(BF)
    da=dA[pl.ds(row,rows),:].astype(F32)
    delta=-jnp.sum(da*a,axis=-1,keepdims=True)*inv
    hi=delta.astype(BF).astype(F32)
    lane=lax.broadcasted_iota(jnp.int32,(rows,hd),1)
    tail=jnp.where(lane==0,hi,jnp.where(lane==1,delta-hi,0.0)).astype(BF)
    das=(da*inv).astype(BF)
    dw=mm(jnp.concatenate([das,tail],axis=1),va[...],1,1)
    ds=(e*dw).astype(BF)
    dq=mm(ds,kn[:,:hd])*scale
    dk=mm(qb[:,:hd],ds,0,0)
    dv=mm(das,eb,0,0)
    dkt[...]+=dk
    dvt[...]+=dv
    dqr=rms_back(qraw[pl.ds(row,rows),:],gq[...],dq,-1)
    gl[0:hd,pl.ds(row,rows)]=jnp.transpose(dqr).astype(BF)

def finish(scale, kraw, gkc, dkt, dvt, gl):
    hd=dkt.shape[0]
    seq=dkt.shape[1]
    step=512
    @pl.loop(0,seq//step)
    def _(i):
        c=pl.multiple_of(i*step,step)
        kt=jnp.transpose(kraw[pl.ds(c,step),:])
        r=rms_back(kt,gkc[...],dkt[:,pl.ds(c,step)]*scale,0)
        gl[hd:2*hd,pl.ds(c,step)]=r.astype(BF)
        gl[2*hd:,pl.ds(c,step)]=dvt[:,pl.ds(c,step)].astype(BF)

def local_kernel(scale, tile_rows, tok_h, cot_h, w, wo, gq, gk, gkc, kb,
                 att_o, g_o, tok, cot, qraw, kraw, qn, kn, va, dA, gl, dkt, dvt, sem):
    seq=tok.shape[0]; hd=gq.shape[1]; R=256; nb=seq//R
    cps=[]
    for j,(h,v) in enumerate(((tok_h,tok),(cot_h,cot))):
        for i in range(nb):
            c=pltpu.make_async_copy(h.at[pl.ds(i*R,R)],v.at[pl.ds(i*R,R)],sem.at[j,i]); c.start(); cps.append(c)
    kn[:,hd:]=kb[...]
    dkt[...]=jnp.zeros_like(dkt); dvt[...]=jnp.zeros_like(dvt)
    for c in cps: c.wait()
    @pl.loop(0,nb)
    def _(i):
        row=pl.multiple_of(i*R,R)
        qkv_block(row,R,tok,w,gq,gk,qraw,kraw,qn,kn,va,tile_rows)
        dA[pl.ds(row,R),:]=mm(cot[pl.ds(row,R),:],wo[...],1,1).astype(BF)
    @pl.loop(0,nb)
    def _(i):
        row=pl.multiple_of(i*R,R)
        attn_block(row,R,None,scale,qn,kn,va,dA,qraw,gq,att_o,gl,dkt,dvt)
    finish(scale,kraw,gkc,dkt,dvt,gl)
    N=256
    @pl.loop(0,tok.shape[1]//N)
    def _(i):
        c=pl.multiple_of(i*N,N)
        g_o[:3*hd,pl.ds(c,N)]=mm(gl[...],tok[:,pl.ds(c,N)]).astype(BF)
        g_o[3*hd:,pl.ds(c,N)]=mm(att_o[...],cot[:,pl.ds(c,N)],0,0).astype(BF)

def local_call(tokens,cot,w,wo,q_gain,k_gain,allowed):
    seq,D=tokens.shape; hd=q_gain.shape[0]
    tile_rows=seq//allowed.shape[0]
    bias=jnp.where(allowed>0.5,0.0,-30000.0).astype(BF)
    kb=jnp.pad(jnp.repeat(bias.T,tile_rows,axis=0),((0,0),(0,hd-allowed.shape[0])))
    V=pl.BlockSpec(memory_space=pltpu.VMEM); A=pl.BlockSpec(memory_space=pl.ANY)
    nb=seq//256
    return pl.pallas_call(functools.partial(local_kernel,hd**-0.5,tile_rows),
      out_shape=(jax.ShapeDtypeStruct((seq,hd),BF),jax.ShapeDtypeStruct((4*hd,D),BF)),
      in_specs=[A,A]+[V]*6, out_specs=(V,V),
      scratch_shapes=[pltpu.VMEM((seq,D),BF)]*2+[pltpu.VMEM((seq,hd),F32)]*2+[pltpu.VMEM((seq,2*hd),BF)]*3
       +[pltpu.VMEM((seq,hd),BF),pltpu.VMEM((3*hd,seq),BF),pltpu.VMEM((hd,seq),F32),pltpu.VMEM((hd,seq),F32),pltpu.SemaphoreType.DMA((2,nb))],
      compiler_params=pltpu.CompilerParams(vmem_limit_bytes=60*1024*1024),
    )(tokens,cot,w,wo,q_gain[None],k_gain[None],k_gain[:,None],kb)


def exchange_kernel(n, att, w, out, rows, send, recv, own):
    me = lax.axis_index("ctx"); dp = lax.axis_index("dp")
    T = rows.shape[0]; hd = att.shape[1]
    bar = pltpu.get_barrier_semaphore()
    def peer(k):
        return lax.rem(me + k, n)
    for k in range(1, n):
        pl.semaphore_signal(bar, inc=1, device_id=(dp, peer(k)), device_id_type=pl.DeviceIdType.MESH)
    pl.semaphore_wait(bar, n - 1)
    def copy(k):
        p = peer(k)
        return pltpu.make_async_remote_copy(
            src_ref=att.at[pl.ds(pl.multiple_of(p * T, T), T)],
            dst_ref=rows.at[:, pl.ds(pl.multiple_of(me * hd, hd), hd)],
            send_sem=send.at[k], recv_sem=recv.at[k],
            device_id=(dp, p), device_id_type=pl.DeviceIdType.MESH)
    for k in range(1, n):
        copy(k).start()
    mine = pltpu.make_async_copy(att.at[pl.ds(pl.multiple_of(me * T, T), T)],
                                 rows.at[:, pl.ds(pl.multiple_of(me * hd, hd), hd)], own)
    mine.start()
    mine.wait()
    for k in range(1, n):
        copy(k).wait()
    out[...] = mm(rows[...], w[...]).astype(BF)


def exchange_call(att, w_full, n):
    seq, hd = att.shape
    V = pl.BlockSpec(memory_space=pltpu.VMEM)
    return pl.pallas_call(functools.partial(exchange_kernel, n),
        out_shape=jax.ShapeDtypeStruct((seq // n, w_full.shape[1]), BF),
        in_specs=[pl.BlockSpec(memory_space=pl.ANY), V], out_specs=V,
        scratch_shapes=[pltpu.VMEM((seq // n, n * hd), BF), pltpu.SemaphoreType.DMA((n,)),
                        pltpu.SemaphoreType.DMA((n,)), pltpu.SemaphoreType.DMA],
        compiler_params=pltpu.CompilerParams(collective_id=1, has_side_effects=True, vmem_limit_bytes=40 * 1024 * 1024),
    )(att, w_full)


def tile_allowed(lists, tile_count):
    match = lists[:, :, None] == jnp.arange(tile_count, dtype=jnp.int32)[None, None, :]
    return jnp.any(match, axis=1).astype(jnp.float32)


def per_device(n, hidden_in, cotangent, w_qkv, w_out, q_gain, k_gain, tile_list):
    tokens = lax.all_gather(hidden_in[0], "ctx", axis=0, tiled=True)
    upstream = lax.all_gather(cotangent[0], "ctx", axis=0, tiled=True)
    w_full = lax.all_gather(w_out, "ctx", axis=0, tiled=True)
    allowed = tile_allowed(tile_list[0], tile_list.shape[1])
    w = jnp.concatenate([w_qkv[0], w_qkv[1], w_qkv[2]], axis=1)
    att, g = local_call(tokens, upstream, w, w_out, q_gain, k_gain, allowed)
    g = lax.psum(g, "dp")
    layer = exchange_call(att, w_full, n)
    hd = q_gain.shape[0]
    gq = g[:3 * hd].reshape(3, hd, -1).transpose(0, 2, 1).astype(F32)
    return layer[None], gq, g[3 * hd:].astype(F32)


def solution(mesh):
    in_specs = (
        P("dp", "ctx", None),
        P("dp", "ctx", None),
        P(None, None, "ctx"),
        P("ctx", None),
        P(),
        P(),
        P("ctx", None, None),
    )
    out_specs = (P("dp", "ctx", None), P(None, None, "ctx"), P("ctx", None))
    return jax.shard_map(
        functools.partial(per_device, mesh.shape["ctx"]), mesh=mesh, in_specs=in_specs, out_specs=out_specs, check_vma=False
    )
```

time: 829 us -> 264 us (0.32)
  local copies, waits for them, and re-layouts: 192 us -> 9.07 us
  blocking collectives: 169 us -> 0 us
  matrix products: 125 us -> 0 us
  other arithmetic: 125 us -> 3.1 us
  Pallas kernels: 0 us -> 55.4 us
  loops' own time: 48.8 us -> 0 us
  waiting for transfers between devices: 149 us -> 183 us
    all_to_all x1 -> x0, blocking collectives: 169 us -> none  [per_device(): lax.all_to_all(as_sent(attention_mine), 'ctx', split_axis=0, concat_axis=...]
    dot_general x65 -> x0, matrix products: 125 us -> none  [the longest x61 105 us: contract(): lax.dot_general(left, right, (((left_dim,), (right_dim,)), ((), ())), pre...]
    another operation x74 -> x0, local copies, waits for them, and re-layouts: 115 us -> none
    pallas_call x0 -> x2, Pallas kernels: none -> 55.4 us  [the longest x1 37.7 us: local_call(): pl.pallas_call(functools.partial(local_kernel, hd ** (-0.5), tile_rows),...]
    another operation x114 -> x0, loops' own time: 48.8 us -> none  [the longest x1 24.2 us: per_device(): lax.scan(backward_step, (zeros, zeros), indices)]
    scatter-add x28 -> x0, other arithmetic: 48.5 us -> none  [the longest x16 27 us: backward_step(): key_grad.at[key_index]]
    reduce_sum x46 -> x0, other arithmetic: 40.7 us -> none  [the longest x40 26.5 us: probabilities_of(): return weighted / jnp.sum(weighted, axis=-1, keepdims=True)]
    all_gather x3, waiting for transfers between devices: 74.9 us -> 100 us  [the longest x1 46.5 us: per_device(): upstream = lax.all_gather(cotangent[0], 'ctx', axis=0, tiled=True)]
  transfers between devices with their start and end apart: 4 -> 4, of which waited for: 3 -> 4; matrix products, arithmetic and copies ran while one was open for 52% -> 2% of each run, Pallas kernels for 0% -> 21%
where the time goes in v1:
time: 264 us
  waiting for transfers between devices  183 us (69%)
  Pallas kernels  55.4 us (21%)
  between operations  13.8 us (5%)
  local copies, waits for them, and re-layouts  9.07 us (3%)
  other arithmetic  3.1 us (1%)
    psum x1, waiting for transfers between devices, per_device(): g = lax.psum(g, 'dp')  80.4 us
    all_gather x1, waiting for transfers between devices, per_device(): upstream = lax.all_gather(cotangent[0], 'ctx', axis=0, tiled=True)  46.5 us
    all_gather x1, waiting for transfers between devices, per_device(): tokens = lax.all_gather(hidden_in[0], 'ctx', axis=0, tiled=True)  44.7 us
    pallas_call x1, Pallas kernels, local_call(): pl.pallas_call(functools.partial(local_kernel, hd ** (-0.5), tile_rows),...  37.7 us
    pallas_call x1, Pallas kernels, exchange_call(): pl.pallas_call(functools.partial(exchange_kernel, n), out_shape=jax.Shape...  17.7 us
    all_gather x1, waiting for transfers between devices, per_device(): w_full = lax.all_gather(w_out, 'ctx', axis=0, tiled=True)  8.79 us
  transfers between devices with their start and end apart: 4, of which 4 were waited for; matrix products, arithmetic and copies ran while one was open for 2% of the time, Pallas kernels for 21%

profile of v1, /device:TPU:2, one launch (start us, length us, event | category | flops | bytes accessed | tf_op | source)
XLA Modules:
  0.0 264.1 jit_solution(12199336372785307092)
XLA Ops:
  7.2 0.0 copy-start.3
  7.2 0.0 all-gather.8.cloned.1.call-start
  7.2 0.7 all-gather.8.cloned.1.call-update
  7.9 0.0 all-gather.10.cloned.1.call-start
  8.0 0.7 all-gather.10.cloned.1.call-update
  8.7 0.0 all-gather.6.cloned.1.call-start
  8.7 0.7 all-gather.6.cloned.1.call-update
  9.4 0.0 all-reduce.3.cloned.1.call-start
  9.4 0.9 fusion
  10.4 0.1 copy.12
  10.5 1.4 copy.13.gkc
  11.9 0.1 broadcast_in_dim.29
  12.0 0.9 pad.4.kb
  12.9 0.0 copy-done.3
  12.9 0.1 slice_bitcast_fusion.2
  12.9 1.2 pad_maximum_fusion.w
  14.1 44.7 %all-gather.8.cloned.1.call-done = bf16[1,2048,1536]{2,1,0:T(8,128)(2,1)} async-done(((bf16[1,128,1536]{2,1,0:T(8,128)(2,1)}), bf16[1,2048,1536]{2,1,0:T(8,128)(2,1)}) %all-gather.8.cloned.1.call-update) | async-done | bytes 6291472 | tf_op jit(solution)/shard_map/all_gather | solution.py:163
  58.9 46.5 %all-gather.10.cloned.1.call-done = bf16[1,2048,1536]{2,1,0:T(8,128)(2,1)} async-done(((bf16[1,128,1536]{2,1,0:T(8,128)(2,1)}), bf16[1,2048,1536]{2,1,0:T(8,128)(2,1)}) %all-gather.10.cloned.1.call-update) | async-done | bytes 6291472 | tf_op jit(solution)/shard_map/all_gather | solution.py:164
  105.4 37.7 %shard_map.94 = (bf16[2048,128]{1,0:T(8,128)(2,1)}, bf16[512,1536]{1,0:T(8,128)(2,1)}) custom-call(bf16[2048,1536]{1,0:T(8,128)(2,1)} %bitcast.20, bf16[2048,1536]{1,0:T(8,128)(2,1)} %bitcast.21, bf16[1536,384]{1,0:T(8,128)(2,1)} %pad_maximum_fusion.w, bf16[128,1536]{1,0:T(8,128)(2,1)} %wo.1, f32[1,128]{1,0:T(1,128)} %bitcast.28, f32[1,128]{1,0:T(1,128)} %bitcast.27, ...), custom_call_target="tpu_custom_call" | custom-call | tf_op jit(solution)/shard_map/pallas_call | solution.py:109
  143.1 0.0 copy-start.1
  143.1 0.0 all-reduce.3.cloned.1.call-update
  143.1 8.8 %all-gather.6.cloned.1.call-done.w = bf16[2048,1536]{1,0:T(8,128)(2,1)} async-done(((bf16[128,1536]{1,0:T(8,128)(2,1)}), bf16[2048,1536]{1,0:T(8,128)(2,1)}) %all-gather.6.cloned.1.call-update) | async-done | bytes 6291472 | tf_op jit(solution)/shard_map/all_gather | solution.py:165
  151.9 0.0 copy-done.1
  151.9 0.0 copy-start
  151.9 2.8 %copy-done = bf16[2048,1536]{1,0:T(8,128)(2,1)S(1)} copy-done((bf16[2048,1536]{1,0:T(8,128)(2,1)S(1)}, bf16[2048,1536]{1,0:T(8,128)(2,1)}, u32[]{:S(2)}) %copy-start) | copy-done | bytes 6291480
  154.7 17.7 %shard_map.95 = bf16[128,1536]{1,0:T(8,128)(2,1)S(1)} custom-call(bf16[2048,128]{1,0:T(8,128)(2,1)S(1)} %copy-done.1, bf16[2048,1536]{1,0:T(8,128)(2,1)S(1)} %copy-done), custom_call_target="tpu_custom_call" | custom-call | tf_op jit(solution)/shard_map/pallas_call | solution.py:148
  172.4 80.4 %all-reduce.3.cloned.1.call-done = bf16[512,1536]{1,0:T(8,128)(2,1)} async-done(((bf16[512,1536]{1,0:T(8,128)(2,1)}), bf16[512,1536]{1,0:T(8,128)(2,1)}) %all-reduce.3.cloned.1.call-update) | async-done | bytes 1572880 | tf_op jit(solution)/shard_map/psum | solution.py:169
  252.9 0.0 slice-start
  252.9 1.3 slice-done
  254.1 0.0 copy-start.2
  254.1 1.7 copy.14
  255.9 0.0 copy-done.2
  255.9 1.0 slice_convert_fusion
  256.8 0.7 copy.17
  (1 shorter events, 0.0 us)
Async XLA Ops:
  7.2 5.7 %copy-start.3 = (bf16[3,1536,128]{2,1,0:T(8,128)(2,1)S(1)}, bf16[3,1536,128]{2,1,0:T(8,128)(2,1)}, u32[]{:S(2)}) copy-start(bf16[3,1536,128]{2,1,0:T(8,128)(2,1)} %param.9) | copy-start | bytes 3538948
  7.2 51.7 %all-gather.8.cloned.1.call-start = ((), (), s32[]{:S(2)}) async-start(), calls=%async_computation.2 | async-start | bytes 6684672 | tf_op jit(solution)/shard_map/all_gather | solution.py:163
  7.9 97.5 %all-gather.10.cloned.1.call-start = ((), (), s32[]{:S(2)}) async-start(), calls=%async_computation.3 | async-start | bytes 6684672 | tf_op jit(solution)/shard_map/all_gather | solution.py:164
  8.7 143.3 %all-gather.6.cloned.1.call-start = ((), (), s32[]{:S(2)}) async-start(), calls=%async_computation | async-start | bytes 6684672 | tf_op jit(solution)/shard_map/all_gather | solution.py:165
  9.4 243.5 %all-reduce.3.cloned.1.call-start = ((), (), s32[]{:S(2)}) async-start(), calls=%async_computation.1 | async-start | bytes 3145728 | tf_op jit(solution)/shard_map/psum | solution.py:169
  143.1 8.8 %copy-start.1 = (bf16[2048,128]{1,0:T(8,128)(2,1)S(1)}, bf16[2048,128]{1,0:T(8,128)(2,1)}, u32[]{:S(2)}) copy-start(bf16[2048,128]{1,0:T(8,128)(2,1)} %get-tuple-element.5.att) | copy-start | bytes 1572868
  151.9 2.8 %copy-start = (bf16[2048,1536]{1,0:T(8,128)(2,1)S(1)}, bf16[2048,1536]{1,0:T(8,128)(2,1)}, u32[]{:S(2)}) copy-start(bf16[2048,1536]{1,0:T(8,128)(2,1)} %all-gather.6.cloned.1.call-done.w) | copy-start | bytes 18874372
  252.9 1.3 slice-start
  254.1 1.7 copy-start.2
Sparse Core Ops, SparseCore 0:
  9.8 48.9 all-gather.7
  60.7 44.6 all-gather.9
  107.2 44.6 all-gather.5
  155.7 97.1 all-reduce.2

commit v2 on v1

--- a/solution.py
+++ b/solution.py
@@ -72,47 +72,172 @@
         gl[hd:2*hd,pl.ds(c,step)]=r.astype(BF)
         gl[2*hd:,pl.ds(c,step)]=dvt[:,pl.ds(c,step)].astype(BF)
 
-def local_kernel(scale, tile_rows, tok_h, cot_h, w, wo, gq, gk, gkc, kb,
-                 att_o, g_o, tok, cot, qraw, kraw, qn, kn, va, dA, gl, dkt, dvt, sem):
-    seq=tok.shape[0]; hd=gq.shape[1]; R=256; nb=seq//R
-    cps=[]
-    for j,(h,v) in enumerate(((tok_h,tok),(cot_h,cot))):
-        for i in range(nb):
-            c=pltpu.make_async_copy(h.at[pl.ds(i*R,R)],v.at[pl.ds(i*R,R)],sem.at[j,i]); c.start(); cps.append(c)
-    kn[:,hd:]=kb[...]
-    dkt[...]=jnp.zeros_like(dkt); dvt[...]=jnp.zeros_like(dvt)
-    for c in cps: c.wait()
-    @pl.loop(0,nb)
+def mesh_copy(src, dst, send, recv, target):
+    return pltpu.make_async_remote_copy(
+        src_ref=src, dst_ref=dst, send_sem=send, recv_sem=recv,
+        device_id=target, device_id_type=pl.DeviceIdType.MESH)
+
+
+def layer_kernel(scale, n, tok_h, cot_h, w3, wo, gq, gk, tiles, att_o, g_o,
+                 tok, cot, w, qraw, kraw, qn, kn, va, dA, gl, dkt, dvt,
+                 ring_send, ring_recv, sib_send, sib_recv, own_send, own_recv, local):
+    chips = n // 2
+    own = tok_h.shape[0]
+    chip = 2 * own
+    half = own // 2
+    events = chips - 1
+    hd = gq.shape[1]
+    tile_rows = tok.shape[0] // tiles.shape[0]
+    me = lax.axis_index("ctx")
+    dp = lax.axis_index("dp")
+    z = me // 2
+    c = me % 2
+    sib = (dp, me + 1 - 2 * c)
+    side = ((dp, lax.rem(me + 2, n)), (dp, lax.rem(me + n - 2, n)))
+    bar = pltpu.get_barrier_semaphore()
+    for t in (sib,) + side:
+        pl.semaphore_signal(bar, inc=1, device_id=t, device_id_type=pl.DeviceIdType.MESH)
+    pl.semaphore_wait(bar, 3)
+
+    def chunk(way, e, core):
+        far = e // 2 + 1
+        part = e % 2
+        origin = lax.rem(z + (chips - far if way == 0 else far), chips)
+        return pl.ds(pl.multiple_of(origin * chip + core * own + (part if way == 0 else 1 - part) * half, half), half)
+
+    heads = (tok_h, cot_h)
+    bufs = (tok, cot)
+
+    def sent(s, way, e):
+        return mesh_copy(bufs[s].at[chunk(way, e - 2, c)], bufs[s].at[chunk(way, e - 2, c)],
+                         ring_send.at[s, way, e], ring_recv.at[s, way, e], side[way])
+
+    def first(s, way, e):
+        h = e if way == 0 else 1 - e
+        return mesh_copy(heads[s].at[pl.ds(h * half, half)],
+                         bufs[s].at[pl.ds(pl.multiple_of(me * own + h * half, half), half)],
+                         ring_send.at[s, way, e], ring_recv.at[s, way, e], side[way])
+
+    def shared(s, way, e):
+        return mesh_copy(bufs[s].at[chunk(way, e, c)], bufs[s].at[chunk(way, e, c)],
+                         sib_send.at[s, way, e], sib_recv.at[s, way, e], sib)
+
+    place = pl.ds(pl.multiple_of(me * own, own), own)
+
+    def lodged(s):
+        return mesh_copy(heads[s], bufs[s].at[place], own_send.at[s], own_recv.at[s], sib)
+
+    def kept(s):
+        return pltpu.make_async_copy(heads[s], bufs[s].at[place], local.at[s])
+
+    def begin(s):
+        for e in (0, 1):
+            for way in (0, 1):
+                first(s, way, e).start()
+        lodged(s).start()
+        kept(s).start()
+
+    def event(s, i):
+        @pl.when(i < events)
+        def _():
+            for way in (0, 1):
+                mesh_copy(bufs[s].at[chunk(way, i, c)], bufs[s].at[chunk(way, i, c)],
+                          ring_send.at[s, way, i], ring_recv.at[s, way, i], side[way]).wait_recv()
+
+                @pl.when(i < events - 2)
+                def _():
+                    sent(s, way, i + 2).start()
+                shared(s, way, i).start()
+
+    def block_row(s, i):
+        far = (i + 1) // 2
+
+        @pl.when(i == 0)
+        def _():
+            lodged(s).wait_recv()
+            kept(s).wait()
+
+        for way in (0, 1):
+            @pl.when(jnp.logical_and(i % 2 == 1 - way, jnp.logical_and(i > 0, i < chips - 1)))
+            def _():
+                shared(s, way, 2 * far - 2).wait_recv()
+                shared(s, way, 2 * far - 1).wait_recv()
+
+            @pl.when(i == chips - 1)
+            def _():
+                shared(s, way, events - 1).wait_recv()
+        zc = lax.rem(z + jnp.where(i % 2 == 1, chips - far, far), chips)
+        return pl.multiple_of(zc * chip, chip)
+
+    begin(0)
+    for j in range(3):
+        w[:, j * hd:(j + 1) * hd] = w3[j]
+    lists = tiles[...]
+    lane = lax.broadcasted_iota(jnp.int32, (hd, hd), 1)
+    count = lists.shape[0]
+    hit = jnp.zeros((count, hd), jnp.bool_)
+    for j in range(lists.shape[1]):
+        hit = jnp.logical_or(hit, lists[:, j:j + 1] == lane[:count])
+    bias = jnp.where(hit, 0.0, -30000.0)
+    bias = jnp.transpose(jnp.concatenate([bias, jnp.zeros((hd - count, hd), F32)], axis=0))
+    for j in range(count):
+        kn[j * tile_rows:(j + 1) * tile_rows, hd:] = jnp.broadcast_to(bias[j:j + 1, :], (tile_rows, hd)).astype(BF)
+    dkt[...] = jnp.zeros_like(dkt)
+    dvt[...] = jnp.zeros_like(dvt)
+
+    @pl.loop(0, chips)
     def _(i):
-        row=pl.multiple_of(i*R,R)
-        qkv_block(row,R,tok,w,gq,gk,qraw,kraw,qn,kn,va,tile_rows)
-        dA[pl.ds(row,R),:]=mm(cot[pl.ds(row,R),:],wo[...],1,1).astype(BF)
-    @pl.loop(0,nb)
+        event(0, i)
+
+        @pl.when(i == events - 3)
+        def _():
+            begin(1)
+        row = block_row(0, i)
+        qkv_block(row, chip, tok, w, gq, gk, qraw, kraw, qn, kn, va, tile_rows)
+
+    @pl.loop(0, chips)
     def _(i):
-        row=pl.multiple_of(i*R,R)
-        attn_block(row,R,None,scale,qn,kn,va,dA,qraw,gq,att_o,gl,dkt,dvt)
-    finish(scale,kraw,gkc,dkt,dvt,gl)
-    N=256
-    @pl.loop(0,tok.shape[1]//N)
+        event(1, i)
+        row = block_row(1, i)
+        dA[pl.ds(row, chip), :] = mm(cot[pl.ds(row, chip), :], wo[...], 1, 1).astype(BF)
+        attn_block(row, chip, None, scale, qn, kn, va, dA, qraw, gq, att_o, gl, dkt, dvt)
+
+    gkc = jnp.transpose(jnp.broadcast_to(gk[...], (hd, hd)))[:, :1]
+    finish(scale, kraw, gkc, dkt, dvt, gl)
+    N = 256
+
+    @pl.loop(0, tok.shape[1] // N)
     def _(i):
-        c=pl.multiple_of(i*N,N)
-        g_o[:3*hd,pl.ds(c,N)]=mm(gl[...],tok[:,pl.ds(c,N)]).astype(BF)
-        g_o[3*hd:,pl.ds(c,N)]=mm(att_o[...],cot[:,pl.ds(c,N)],0,0).astype(BF)
-
-def local_call(tokens,cot,w,wo,q_gain,k_gain,allowed):
-    seq,D=tokens.shape; hd=q_gain.shape[0]
-    tile_rows=seq//allowed.shape[0]
-    bias=jnp.where(allowed>0.5,0.0,-30000.0).astype(BF)
-    kb=jnp.pad(jnp.repeat(bias.T,tile_rows,axis=0),((0,0),(0,hd-allowed.shape[0])))
-    V=pl.BlockSpec(memory_space=pltpu.VMEM); A=pl.BlockSpec(memory_space=pl.ANY)
-    nb=seq//256
-    return pl.pallas_call(functools.partial(local_kernel,hd**-0.5,tile_rows),
-      out_shape=(jax.ShapeDtypeStruct((seq,hd),BF),jax.ShapeDtypeStruct((4*hd,D),BF)),
-      in_specs=[A,A]+[V]*6, out_specs=(V,V),
-      scratch_shapes=[pltpu.VMEM((seq,D),BF)]*2+[pltpu.VMEM((seq,hd),F32)]*2+[pltpu.VMEM((seq,2*hd),BF)]*3
-       +[pltpu.VMEM((seq,hd),BF),pltpu.VMEM((3*hd,seq),BF),pltpu.VMEM((hd,seq),F32),pltpu.VMEM((hd,seq),F32),pltpu.SemaphoreType.DMA((2,nb))],
-      compiler_params=pltpu.CompilerParams(vmem_limit_bytes=60*1024*1024),
-    )(tokens,cot,w,wo,q_gain[None],k_gain[None],k_gain[:,None],kb)
+        col = pl.multiple_of(i * N, N)
+        g_o[:3 * hd, pl.ds(col, N)] = mm(gl[...], tok[:, pl.ds(col, N)]).astype(BF)
+        g_o[3 * hd:, pl.ds(col, N)] = mm(att_o[...], cot[:, pl.ds(col, N)], 0, 0).astype(BF)
+
+    for s in (0, 1):
+        lodged(s).wait_send()
+        for way in (0, 1):
+            for e in range(events):
+                (first if e < 2 else sent)(s, way, e).wait_send()
+                shared(s, way, e).wait_send()
+
+
+def layer_call(n, hidden, cot, w3, wo, q_gain, k_gain, tiles):
+    own, D = hidden.shape
+    seq = own * n
+    hd = q_gain.shape[0]
+    V = pl.BlockSpec(memory_space=pltpu.VMEM)
+    A = pl.BlockSpec(memory_space=pl.ANY)
+    dma = pltpu.SemaphoreType.DMA
+    e = n // 2 - 1
+    return pl.pallas_call(
+        functools.partial(layer_kernel, hd ** -0.5, n),
+        out_shape=(jax.ShapeDtypeStruct((seq, hd), BF), jax.ShapeDtypeStruct((4 * hd, D), BF)),
+        in_specs=[A, A] + [V] * 5, out_specs=(V, V),
+        scratch_shapes=[pltpu.VMEM((seq, D), BF)] * 2 + [pltpu.VMEM((D, 3 * hd), BF)]
+        + [pltpu.VMEM((seq, hd), F32)] * 2 + [pltpu.VMEM((seq, 2 * hd), BF)] * 3
+        + [pltpu.VMEM((seq, hd), BF), pltpu.VMEM((3 * hd, seq), BF)] + [pltpu.VMEM((hd, seq), F32)] * 2
+        + [dma((2, 2, e))] * 4 + [dma((2,))] * 3,
+        compiler_params=pltpu.CompilerParams(collective_id=2, has_side_effects=True, vmem_limit_bytes=60 * 1024 * 1024),
+    )(hidden, cot, w3, wo, q_gain[None], k_gain[None], tiles)
 
 
 def exchange_kernel(n, att, w, out, rows, send, recv, own):
@@ -154,18 +279,9 @@
     )(att, w_full)
 
 
-def tile_allowed(lists, tile_count):
-    match = lists[:, :, None] == jnp.arange(tile_count, dtype=jnp.int32)[None, None, :]
-    return jnp.any(match, axis=1).astype(jnp.float32)
-
-
 def per_device(n, hidden_in, cotangent, w_qkv, w_out, q_gain, k_gain, tile_list):
-    tokens = lax.all_gather(hidden_in[0], "ctx", axis=0, tiled=True)
-    upstream = lax.all_gather(cotangent[0], "ctx", axis=0, tiled=True)
     w_full = lax.all_gather(w_out, "ctx", axis=0, tiled=True)
-    allowed = tile_allowed(tile_list[0], tile_list.shape[1])
-    w = jnp.concatenate([w_qkv[0], w_qkv[1], w_qkv[2]], axis=1)
-    att, g = local_call(tokens, upstream, w, w_out, q_gain, k_gain, allowed)
+    att, g = layer_call(n, hidden_in[0], cotangent[0], w_qkv, w_out, q_gain, k_gain, tile_list[0])
     g = lax.psum(g, "dp")
     layer = exchange_call(att, w_full, n)
     hd = q_gain.shape[0]

time: 264 us -> 224 us (0.85)
  waiting for transfers between devices: 183 us -> 98.4 us
  Pallas kernels: 55.4 us -> 100 us
    all_gather x2 -> x0, waiting for transfers between devices: 91.3 us -> none  [the longest x1 46.5 us: per_device(): upstream = lax.all_gather(cotangent[0], 'ctx', axis=0, tiled=True)]
    pallas_call x1, Pallas kernels: 37.7 us -> 80.8 us  [layer_call(): pl.pallas_call(functools.partial(layer_kernel, hd ** (-0.5), n), out_shap...]
    psum x1, waiting for transfers between devices: 80.4 us -> 97.9 us  [per_device(): g = lax.psum(g, 'dp')]
    all_gather x1, waiting for transfers between devices: 8.79 us -> 0.01 us  [per_device(): w_full = lax.all_gather(w_out, 'ctx', axis=0, tiled=True)]
  transfers between devices with their start and end apart: 4 -> 2, of which waited for: 4 -> 1; matrix products, arithmetic and copies ran while one was open for 2% -> 1% of each run, Pallas kernels for 21% -> 0%
where the time goes in v2:
time: 224 us; the launch traced here: 222 us
  Pallas kernels  100 us (45%)
  waiting for transfers between devices  98.4 us (44%)
  between operations  15.5 us (7%)
  local copies, waits for them, and re-layouts  6.54 us (3%)
    psum x1, waiting for transfers between devices, per_device(): g = lax.psum(g, 'dp')  97.9 us
    pallas_call x1, Pallas kernels, layer_call(): pl.pallas_call(functools.partial(layer_kernel, hd ** (-0.5), n), out_shap...  80.8 us
    pallas_call x1, Pallas kernels, exchange_call(): pl.pallas_call(functools.partial(exchange_kernel, n), out_shape=jax.Shape...  19.5 us
  transfers between devices with their start and end apart: 2, of which 1 were waited for; matrix products, arithmetic and copies ran while one was open for 1% of the time, Pallas kernels for 0%

profile of v2, /device:TPU:2, one launch (start us, length us, event | category | flops | bytes accessed | tf_op | source)
XLA Modules:
  0.0 221.8 jit_solution(9611707323926113734)
XLA Ops:
  8.0 0.0 all-reduce.2.cloned.1.call-start
  8.0 80.8 %shard_map.94 = (bf16[2048,128]{1,0:T(8,128)(2,1)}, bf16[512,1536]{1,0:T(8,128)(2,1)}) custom-call(bf16[128,1536]{1,0:T(8,128)(2,1)} %bitcast.12, bf16[128,1536]{1,0:T(8,128)(2,1)} %bitcast.13, bf16[3,1536,128]{2,1,0:T(8,128)(2,1)} %w3.1, bf16[128,1536]{1,0:T(8,128)(2,1)} %wo.1, f32[1,128]{1,0:T(1,128)} %bitcast.15, f32[1,128]{1,0:T(1,128)} %bitcast.16, ...), custom_call_target="tpu_custom_call" | custom-call | tf_op jit(solution)/shard_map/pallas_call | solution.py:231
  88.8 0.0 all-reduce.2.cloned.1.call-update
  88.9 0.0 all-gather.2.cloned.1.call-start
  88.9 0.5 all-gather.2.cloned.1.call-update
  89.4 97.9 %all-reduce.2.cloned.1.call-done = bf16[512,1536]{1,0:T(8,128)(2,1)} async-done(((bf16[512,1536]{1,0:T(8,128)(2,1)}), bf16[512,1536]{1,0:T(8,128)(2,1)}) %all-reduce.2.cloned.1.call-update) | async-done | bytes 1572880 | tf_op jit(solution)/shard_map/psum | solution.py:285
  187.3 0.0 slice-start
  187.3 1.3 slice-done
  188.6 0.0 copy-start.2
  188.6 0.0 copy-start.1
  188.6 1.7 copy.10
  190.4 0.0 copy-done.2
  190.4 1.0 slice_convert_fusion
  191.3 0.0 all-gather.2.cloned.1.call-done.w
  191.3 0.0 copy-done.1
  191.3 0.0 copy-start
  191.3 2.8 %copy-done = bf16[2048,1536]{1,0:T(8,128)(2,1)S(1)} copy-done((bf16[2048,1536]{1,0:T(8,128)(2,1)S(1)}, bf16[2048,1536]{1,0:T(8,128)(2,1)}, u32[]{:S(2)}) %copy-start) | copy-done | bytes 6291480
  194.1 19.5 %shard_map.95 = bf16[128,1536]{1,0:T(8,128)(2,1)S(1)} custom-call(bf16[2048,128]{1,0:T(8,128)(2,1)S(1)} %copy-done.1, bf16[2048,1536]{1,0:T(8,128)(2,1)S(1)} %copy-done), custom_call_target="tpu_custom_call" | custom-call | tf_op jit(solution)/shard_map/pallas_call | solution.py:273
  213.6 0.7 copy.13
Async XLA Ops:
  8.0 179.3 %all-reduce.2.cloned.1.call-start = ((), (), s32[]{:S(2)}) async-start(), calls=%async_computation.1 | async-start | bytes 3145728 | tf_op jit(solution)/shard_map/psum | solution.py:285
  88.9 102.5 %all-gather.2.cloned.1.call-start = ((), (), s32[]{:S(2)}) async-start(), calls=%async_computation | async-start | bytes 6684672 | tf_op jit(solution)/shard_map/all_gather | solution.py:283
  187.3 1.3 slice-start
  188.6 1.7 copy-start.2
  188.6 2.7 %copy-start.1 = (bf16[2048,128]{1,0:T(8,128)(2,1)S(1)}, bf16[2048,128]{1,0:T(8,128)(2,1)}, u32[]{:S(2)}) copy-start(bf16[2048,128]{1,0:T(8,128)(2,1)} %get-tuple-element.5.att) | copy-start | bytes 1572868
  191.3 2.8 %copy-start = (bf16[2048,1536]{1,0:T(8,128)(2,1)S(1)}, bf16[2048,1536]{1,0:T(8,128)(2,1)}, u32[]{:S(2)}) copy-start(bf16[2048,1536]{1,0:T(8,128)(2,1)} %all-gather.2.cloned.1.call-done.w) | copy-start | bytes 18874372
Sparse Core Ops, SparseCore 0:
  89.0 98.3 all-reduce.1
Sparse Core Ops, SparseCore 1:
  91.2 45.8 all-gather.1

commit v3 on v2

--- a/solution.py
+++ b/solution.py
@@ -240,15 +240,27 @@
     )(hidden, cot, w3, wo, q_gain[None], k_gain[None], tiles)
 
 
-def exchange_kernel(n, att, w, out, rows, send, recv, own):
+def exchange_kernel(n, m, att, w, g, out, gq_o, go_o, rows, send, recv, own, parts, full, rs_send, rs_recv, ag_send, ag_recv, gown):
     me = lax.axis_index("ctx"); dp = lax.axis_index("dp")
     T = rows.shape[0]; hd = att.shape[1]
+    R = full.shape[0] // m
     bar = pltpu.get_barrier_semaphore()
     def peer(k):
         return lax.rem(me + k, n)
+    def dpeer(k):
+        return lax.rem(dp + k, m)
+    for k in range(1, m):
+        pl.semaphore_signal(bar, inc=1, device_id=(dpeer(k), me), device_id_type=pl.DeviceIdType.MESH)
     for k in range(1, n):
         pl.semaphore_signal(bar, inc=1, device_id=(dp, peer(k)), device_id_type=pl.DeviceIdType.MESH)
-    pl.semaphore_wait(bar, n - 1)
+    pl.semaphore_wait(bar, n + m - 2)
+    def band(p):
+        return pl.ds(pl.multiple_of(p * R, R), R)
+    def scatter(k):
+        p = dpeer(k)
+        return mesh_copy(g.at[band(p)], parts.at[k], rs_send.at[k], rs_recv.at[k], (p, me))
+    def gather(k):
+        return mesh_copy(full.at[band(dp)], full.at[band(dp)], ag_send.at[k], ag_recv.at[k], (dpeer(k), me))
     def copy(k):
         p = peer(k)
         return pltpu.make_async_remote_copy(
@@ -256,37 +268,59 @@
             dst_ref=rows.at[:, pl.ds(pl.multiple_of(me * hd, hd), hd)],
             send_sem=send.at[k], recv_sem=recv.at[k],
             device_id=(dp, p), device_id_type=pl.DeviceIdType.MESH)
+    for k in range(1, m):
+        scatter(k).start()
     for k in range(1, n):
         copy(k).start()
     mine = pltpu.make_async_copy(att.at[pl.ds(pl.multiple_of(me * T, T), T)],
                                  rows.at[:, pl.ds(pl.multiple_of(me * hd, hd), hd)], own)
     mine.start()
+    keep = pltpu.make_async_copy(g.at[band(dp)], parts.at[0], gown)
+    keep.start()
+    keep.wait()
+    total = parts[0].astype(F32)
+    for k in range(1, m):
+        scatter(k).wait_recv()
+        total = total + parts[k].astype(F32)
+    full[band(dp), :] = total.astype(BF)
+    for k in range(1, m):
+        gather(k).start()
     mine.wait()
     for k in range(1, n):
         copy(k).wait()
     out[...] = mm(rows[...], w[...]).astype(BF)
-
-
-def exchange_call(att, w_full, n):
+    for k in range(1, m):
+        gather(k).wait_recv()
+    for j in range(3):
+        gq_o[j] = jnp.transpose(full[j * hd:(j + 1) * hd, :].astype(F32))
+    go_o[...] = full[3 * hd:, :].astype(F32)
+    for k in range(1, m):
+        scatter(k).wait_send()
+        gather(k).wait_send()
+
+
+def exchange_call(att, w_full, g, n, m):
     seq, hd = att.shape
+    D = w_full.shape[1]
     V = pl.BlockSpec(memory_space=pltpu.VMEM)
-    return pl.pallas_call(functools.partial(exchange_kernel, n),
-        out_shape=jax.ShapeDtypeStruct((seq // n, w_full.shape[1]), BF),
-        in_specs=[pl.BlockSpec(memory_space=pl.ANY), V], out_specs=V,
-        scratch_shapes=[pltpu.VMEM((seq // n, n * hd), BF), pltpu.SemaphoreType.DMA((n,)),
-                        pltpu.SemaphoreType.DMA((n,)), pltpu.SemaphoreType.DMA],
+    A = pl.BlockSpec(memory_space=pl.ANY)
+    dma = pltpu.SemaphoreType.DMA
+    return pl.pallas_call(functools.partial(exchange_kernel, n, m),
+        out_shape=(jax.ShapeDtypeStruct((seq // n, D), BF), jax.ShapeDtypeStruct((3, D, hd), F32),
+                   jax.ShapeDtypeStruct((hd, D), F32)),
+        in_specs=[A, V, A], out_specs=(V, V, V),
+        scratch_shapes=[pltpu.VMEM((seq // n, n * hd), BF), dma((n,)), dma((n,)), dma,
+                        pltpu.VMEM((m, 4 * hd // m, D), BF), pltpu.VMEM((4 * hd, D), BF)]
+        + [dma((m,))] * 4 + [dma],
         compiler_params=pltpu.CompilerParams(collective_id=1, has_side_effects=True, vmem_limit_bytes=40 * 1024 * 1024),
-    )(att, w_full)
-
-
-def per_device(n, hidden_in, cotangent, w_qkv, w_out, q_gain, k_gain, tile_list):
+    )(att, w_full, g)
+
+
+def per_device(n, m, hidden_in, cotangent, w_qkv, w_out, q_gain, k_gain, tile_list):
     w_full = lax.all_gather(w_out, "ctx", axis=0, tiled=True)
     att, g = layer_call(n, hidden_in[0], cotangent[0], w_qkv, w_out, q_gain, k_gain, tile_list[0])
-    g = lax.psum(g, "dp")
-    layer = exchange_call(att, w_full, n)
-    hd = q_gain.shape[0]
-    gq = g[:3 * hd].reshape(3, hd, -1).transpose(0, 2, 1).astype(F32)
-    return layer[None], gq, g[3 * hd:].astype(F32)
+    layer, gq, go = exchange_call(att, w_full, g, n, m)
+    return layer[None], gq, go
 
 
 def solution(mesh):
@@ -301,5 +335,5 @@
     )
     out_specs = (P("dp", "ctx", None), P(None, None, "ctx"), P("ctx", None))
     return jax.shard_map(
-        functools.partial(per_device, mesh.shape["ctx"]), mesh=mesh, in_specs=in_specs, out_specs=out_specs, check_vma=False
+        functools.partial(per_device, mesh.shape["ctx"], mesh.shape["dp"]), mesh=mesh, in_specs=in_specs, out_specs=out_specs, check_vma=False
     )

time: 224 us -> 195 us (0.87)
  the two profiles are of different devices: /device:TPU:2 before, /device:TPU:152 now
where the time goes in v3:
time: 195 us
  Pallas kernels  172 us (88%)
  between operations  14.1 us (7%)
  local copies, waits for them, and re-layouts  8.26 us (4%)
    pallas_call x1, Pallas kernels, layer_call(): pl.pallas_call(functools.partial(layer_kernel, hd ** (-0.5), n), out_shap...  107 us
    pallas_call x1, Pallas kernels, exchange_call(): pl.pallas_call(functools.partial(exchange_kernel, n, m), out_shape=(jax.S...  65.1 us
    unnamed x9, local copies, waits for them, and re-layouts  8.26 us
  transfers between devices with their start and end apart: 1, of which 0 were waited for; matrix products, arithmetic and copies ran while one was open for 0% of the time, Pallas kernels for 55%

profile of v3, /device:TPU:152, one launch (start us, length us, event | category | flops | bytes accessed | tf_op | source)
XLA Modules:
  0.0 194.8 jit_solution(604819591111256694)
XLA Ops:
  7.2 0.0 all-gather.2.cloned.1.call-start
  7.2 0.7 all-gather.2.cloned.1.call-update
  7.9 106.7 %shard_map.94 = (bf16[2048,128]{1,0:T(8,128)(2,1)}, bf16[512,1536]{1,0:T(8,128)(2,1)}) custom-call(bf16[128,1536]{1,0:T(8,128)(2,1)} %bitcast.7, bf16[128,1536]{1,0:T(8,128)(2,1)} %bitcast.8, bf16[3,1536,128]{2,1,0:T(8,128)(2,1)} %w3.1, bf16[128,1536]{1,0:T(8,128)(2,1)} %wo.1, f32[1,128]{1,0:T(1,128)} %bitcast.10, f32[1,128]{1,0:T(1,128)} %bitcast.11, ...), custom_call_target="tpu_custom_call" | custom-call | tf_op jit(solution)/shard_map/pallas_call | solution.py:231
  114.6 0.0 all-gather.2.cloned.1.call-done.w
  114.6 0.0 copy-start
  114.6 2.8 %copy-done = bf16[2048,1536]{1,0:T(8,128)(2,1)S(1)} copy-done((bf16[2048,1536]{1,0:T(8,128)(2,1)S(1)}, bf16[2048,1536]{1,0:T(8,128)(2,1)}, u32[]{:S(2)}) %copy-start) | copy-done | bytes 6291480
  117.4 0.0 copy-start.1
  117.4 1.4 copy-done.1
  118.8 0.0 copy-start.2
  118.8 1.0 copy-done.2
  119.8 65.1 %shard_map.95 = (bf16[128,1536]{1,0:T(8,128)(2,1)S(1)}, f32[3,1536,128]{2,1,0:T(8,128)S(1)}, f32[128,1536]{1,0:T(8,128)S(1)}) custom-call(bf16[2048,128]{1,0:T(8,128)(2,1)S(1)} %copy-done.2, bf16[2048,1536]{1,0:T(8,128)(2,1)S(1)} %copy-done, bf16[512,1536]{1,0:T(8,128)(2,1)S(1)} %copy-done.1), custom_call_target="tpu_custom_call" | custom-call | tf_op jit(solution)/shard_map/pallas_call | solution.py:308
  184.9 0.7 copy.13
  185.7 1.4 copy.14
  187.1 0.9 copy.15
Async XLA Ops:
  7.2 107.4 %all-gather.2.cloned.1.call-start = ((), (), s32[]{:S(2)}) async-start(), calls=%async_computation | async-start | bytes 6684672 | tf_op jit(solution)/shard_map/all_gather | solution.py:320
  114.6 2.8 %copy-start = (bf16[2048,1536]{1,0:T(8,128)(2,1)S(1)}, bf16[2048,1536]{1,0:T(8,128)(2,1)}, u32[]{:S(2)}) copy-start(bf16[2048,1536]{1,0:T(8,128)(2,1)} %all-gather.2.cloned.1.call-done.w) | copy-start | bytes 18874372
  117.4 1.4 copy-start.1
  118.8 1.0 copy-start.2
Sparse Core Ops, SparseCore 0:
  9.8 74.1 all-gather.1
